TPU v7x, 128 devices: a whole 4x4x4 slice. The times are simulated.
128 devices in a mesh: grp: 32 (over y_lo, z, x), blk: 4 (over y_hi, core).
Axes of the slice: x: 4, y: 4 (y_hi: 2, y_lo: 2; y = y_hi * 2 + y_lo), z: 4, core: 2. Of those that a mesh axis runs over, the one named last changes fastest.
Arguments:
- embeddings: bfloat16 [196608, 768], P(('grp', 'blk')), may hold values from -6 to 6
- route: int32 [196608], P(('grp', 'blk')), may hold values from 0 to 196607, as said below
- cluster: int32 [32, 6144], P('grp', 'blk'), may hold values from 0 to 3, never falling along the last dimension, each value on 1 to 3072 neighbouring positions
Outputs:
- best_cosine: float32 [196608], P(('grp', 'blk'))
Inputs may be any that keep to these rules, and one draw needn't show every extreme that they name: route is a permutation of all slots; the 1536 rows of each device are sent to every device's 1536 slots in exactly 12 cases, and which rows and which slots is drawn from the seed. Within each family the cluster numbers never fall along the slots, every cluster number occurs, and one cluster has exactly 3072 slots.
All inputs are finite; a program needn't handle non-finite values.
Results may differ from a plain program's by a relative error of at most 0.0014.
Values may be sent and summed in bfloat16 or wider, within the bound.
A program may use at most 64 MiB of HBM per device.

v0:
```python
import jax
import jax.numpy as jnp
from jax import lax
from jax.sharding import PartitionSpec as P


def passed_along(shard, axis, by):
    size = lax.axis_size(axis)
    return lax.ppermute(shard, axis, [(i, (i + by) % size) for i in range(size)])


def fold_tile(best_score, mine, other):
    unit_rows, index_rows, cluster_rows = mine
    unit_other, index_other, cluster_other = other
    row_count = unit_rows.shape[0]
    block_rows = min(512, row_count)
    block_count = row_count // block_rows

    def one_block(packed):
        unit_part, index_part, cluster_part, best_part = packed
        scores = lax.dot_general(
            unit_part, unit_other, (((1,), (1,)), ((), ())), preferred_element_type=jnp.float32
        )
        matches = (cluster_part[:, None] == cluster_other[None, :]) & (
            index_other[None, :] < index_part[:, None]
        )
        return jnp.maximum(best_part, jnp.max(jnp.where(matches, scores, -1.0), axis=1))

    result = lax.map(
        one_block,
        (
            unit_rows.reshape(block_count, block_rows, -1),
            index_rows.reshape(block_count, block_rows),
            cluster_rows.reshape(block_count, block_rows),
            best_score.reshape(block_count, block_rows),
        ),
    )
    return result.reshape(row_count)


def on_device(embeddings, route, cluster):
    row_count, width = embeddings.shape
    device_count = lax.axis_size(("grp", "blk"))
    cycle_size = lax.axis_size("blk")
    pair_rows = row_count // device_count
    here = lax.axis_index(("grp", "blk"))
    data_index = here * row_count + jnp.arange(row_count, dtype=jnp.int32)
    values = embeddings.astype(jnp.float32)
    unit_rows = (
        values * lax.rsqrt(jnp.sum(values * values, axis=1, keepdims=True) + 1e-06)
    ).astype(jnp.bfloat16)
    ordering = jnp.argsort(route)
    sent_unit = jnp.take(unit_rows, ordering, axis=0)
    sent_slot = jnp.take(route % row_count, ordering)
    sent_index = jnp.take(data_index, ordering)
    arrived = (
        lax.all_to_all(
            sent_unit.reshape(device_count, pair_rows, width),
            ("grp", "blk"),
            split_axis=0,
            concat_axis=0,
            tiled=True,
        ),
        lax.all_to_all(
            sent_slot.reshape(device_count, pair_rows),
            ("grp", "blk"),
            split_axis=0,
            concat_axis=0,
            tiled=True,
        ),
        lax.all_to_all(
            sent_index.reshape(device_count, pair_rows),
            ("grp", "blk"),
            split_axis=0,
            concat_axis=0,
            tiled=True,
        ),
    )
    slot_pos = arrived[1].reshape(-1)
    block_unit = (
        jnp.zeros((row_count, width), jnp.bfloat16).at[slot_pos].set(arrived[0].reshape(-1, width))
    )
    block_index = jnp.zeros((row_count,), jnp.int32).at[slot_pos].set(arrived[2].reshape(-1))
    block_cluster = cluster.reshape(-1)
    mine = (block_unit, block_index, block_cluster)
    best_score = jnp.full((row_count,), -1.0, jnp.float32)
    best_score = fold_tile(best_score, mine, mine)
    current = mine
    for stepping in range(cycle_size - 1):
        current = passed_along((current[0], current[1], current[2]), "blk", 1)
        best_score = fold_tile(best_score, mine, current)
    ordering_back = jnp.argsort(block_index)
    home_score = jnp.take(best_score, ordering_back)
    home_pos = jnp.take(block_index % row_count, ordering_back)
    returned = (
        lax.all_to_all(
            home_score.reshape(device_count, pair_rows),
            ("grp", "blk"),
            split_axis=0,
            concat_axis=0,
            tiled=True,
        ),
        lax.all_to_all(
            home_pos.reshape(device_count, pair_rows),
            ("grp", "blk"),
            split_axis=0,
            concat_axis=0,
            tiled=True,
        ),
    )
    return (
        jnp.zeros((row_count,), jnp.float32)
        .at[returned[1].reshape(-1)]
        .set(returned[0].reshape(-1))
    )


def solution(mesh):
    in_specs = (P(("grp", "blk"), None), P(("grp", "blk")), P("grp", "blk"))
    out_specs = P(("grp", "blk"))
    return jax.shard_map(
        on_device, mesh=mesh, in_specs=in_specs, out_specs=out_specs, check_vma=False
    )
```

profile of v0, /device:TPU:13, one launch (start us, length us, event | category | flops | bytes accessed | tf_op | source)
XLA Modules:
  0.0 271.5 jit_solution(12553058925467509926)
XLA Ops:
  0.0 0.7 add_select_fusion.1
  0.7 5.7 %sort.31 = (s32[1536]{0:T(1024)}, s32[1536]{0:T(1024)S(1)}) sort(s32[1536]{0:T(1024)} %param.14, s32[1536]{0:T(1024)S(1)} %iota.10), dimensions={0}, to_apply=%region_0.0 | sort | flops 16896 | bytes 24576 | tf_op jit(solution)/shard_map/jit(argsort)/sort | solution.py:52
  6.5 8.4 %gather_fusion.3 = s32[1536]{0:T(1024)S(1)} fusion(s32[1536]{0:T(1024)S(1)} %iota_add_fusion, s32[2048]{0:T(1024)S(1)} %pad_clamp_fusion.1), kind=kCustom, calls=%fused_computation.1.clone | custom fusion | bytes 18432 | tf_op jit(solution)/shard_map/jit(_take)/gather | solution.py:55
  14.9 8.4 %gather_fusion.2 = s32[1536]{0:T(1024)S(1)} fusion(s32[1536]{0:T(1024)S(1)} %add_select_fusion.1, s32[2048]{0:T(1024)S(1)} %pad_clamp_fusion.1), kind=kCustom, calls=%fused_computation.clone | custom fusion | bytes 18432 | tf_op jit(solution)/shard_map/jit(_take)/gather | solution.py:54
  23.3 0.7 all_to_all.25
  24.0 10.7 %all-to-all-start = ((s32[128,1,12]{2,1,0:T(1,128)}), s32[128,1,12]{2,1,0:T(1,128)S(1)}, u32[]{:S(2)}, u32[]{:S(2)}) async-start(s32[128,1,12]{2,1,0:T(1,128)} %bitcast.16), calls=%async_computation | async-start | bytes 131072 | tf_op jit(solution)/shard_map/all_to_all | solution.py:64
  34.7 0.1 broadcast_in_dim.73
  34.9 0.5 fusion.16
  35.4 1.1 copy-done.1
  36.5 0.4 fusion.17
  37.0 5.7 %gather_fusion = bf16[1536,768]{1,0:T(8,128)(2,1)} fusion(bf16[1536,768]{1,0:T(8,128)(2,1)S(1)} %fusion.17, s32[2048]{0:T(1024)S(1)} %pad_clamp_fusion.1), kind=kCustom, calls=%fused_computation.3 | custom fusion | bytes 4724736 | tf_op jit(solution)/shard_map/jit(_take)/gather | solution.py:53
  42.7 3.4 %gather.14 = bf16[128,12,768]{2,1,0:T(8,128)(2,1)S(1)} reshape(bf16[1536,768]{1,0:T(8,128)(2,1)} %gather_fusion) | data formatting | bytes 4718592 | tf_op jit(solution)/shard_map/jit(_take)/gather | solution.py:53
  46.1 1.9 broadcast_select_fusion
  48.0 9.8 %all-to-all-start.3 = ((bf16[128,12,768]{2,1,0:T(8,128)(2,1)}), bf16[128,12,768]{2,1,0:T(8,128)(2,1)S(1)}, u32[]{:S(2)}, u32[]{:S(2)}) async-start(bf16[128,12,768]{2,1,0:T(8,128)(2,1)} %broadcast_select_fusion), calls=%async_computation.3 | async-start | bytes 6291456 | tf_op jit(solution)/shard_map/all_to_all | solution.py:57
  57.8 0.5 broadcast.136
  58.3 0.7 reduce.19
  59.1 0.1 reshape.193
  59.2 38.9 %all-to-all-done.3 = bf16[128,12,768]{2,1,0:T(8,128)(2,1)S(1)} async-done(((bf16[128,12,768]{2,1,0:T(8,128)(2,1)}), bf16[128,12,768]{2,1,0:T(8,128)(2,1)S(1)}, u32[]{:S(2)}, u32[]{:S(2)}) %all-to-all-start.3) | async-done | bytes 2359328 | tf_op jit(solution)/shard_map/all_to_all | solution.py:57
  98.1 2.1 reshape.254
  100.3 8.7 %scatter_custom_fusion.1 = bf16[1536,768]{1,0:T(8,128)(2,1)S(1)} fusion(s32[1536]{0:T(1024)S(1)} %fusion.20, bf16[1536,768]{1,0:T(8,128)(2,1)} %reshape.254, bf16[]{:T(256)} %constant.131.clone.1), kind=kCustom, calls=%fused_computation.45 | custom fusion | bytes 2359808 | tf_op jit(solution)/shard_map/scatter | solution.py:81
  109.0 1.4 collective-permute-start.2
  110.4 0.7 all_to_all.27
  111.1 8.0 %all-to-all-start.1 = ((s32[128,1,12]{2,1,0:T(1,128)}), s32[128,1,12]{2,1,0:T(1,128)S(1)}, u32[]{:S(2)}, u32[]{:S(2)}) async-start(s32[128,1,12]{2,1,0:T(1,128)} %bitcast.17), calls=%async_computation.1 | async-start | bytes 131072 | tf_op jit(solution)/shard_map/all_to_all | solution.py:71
  119.2 2.4 collective-permute-start
  121.5 18.5 %all-to-all-done.1 = s32[128,1,12]{2,1,0:T(1,128)S(1)} async-done(((s32[128,1,12]{2,1,0:T(1,128)}), s32[128,1,12]{2,1,0:T(1,128)S(1)}, u32[]{:S(2)}, u32[]{:S(2)}) %all-to-all-start.1) | async-done | bytes 6176 | tf_op jit(solution)/shard_map/all_to_all | solution.py:71
  140.1 0.7 reduce.20
  140.8 0.1 reshape.246
  140.9 6.2 %scatter_custom_fusion = s32[1536]{0:T(1024)S(1)} fusion(s32[1536]{0:T(1024)S(1)} %fusion.20, s32[1536]{0:T(1024)S(1)} %reshape.246, s32[]{:T(128)} %constant.124.clone.1), kind=kCustom, calls=%fused_computation.65 | custom fusion | bytes 6148 | tf_op jit(solution)/shard_map/scatter | solution.py:83
  147.1 1.6 collective-permute-start.1
  148.7 5.0 %sort.32 = (s32[1536]{0:T(1024)}, s32[1536]{0:T(1024)S(1)}) sort(s32[1536]{0:T(1024)S(1)} %scatter_custom_fusion, s32[1536]{0:T(1024)S(1)} %iota.12), dimensions={0}, to_apply=%region_2.4 | sort | flops 16896 | bytes 24576 | tf_op jit(solution)/shard_map/jit(argsort)/sort | solution.py:92
  153.9 2.4 collective-permute-start.4
  156.4 8.4 %gather_fusion.4 = s32[1536]{0:T(1024)S(1)} fusion(s32[1536]{0:T(1024)S(1)} %add_select_fusion, s32[2048]{0:T(1024)S(1)} %pad_clamp_fusion), kind=kCustom, calls=%fused_computation.2.clone | custom fusion | bytes 18432 | tf_op jit(solution)/shard_map/jit(_take)/gather | solution.py:94
  164.8 1.3 collective-permute-start.6
  166.2 5.3 %while.40 = (s32[]{:T(128)}, f32[3,512]{1,0:T(4,128)S(1)}, s32[3,512]{1,0:T(4,128)S(1)}, s32[1,1536]{1,0:T(1,128)S(1)}, s32[1536]{0:T(1024)S(1)}, /*index=5*/s32...) while((s32[]{:T(128)}, f32[3,512]{1,0:T(4,128)S(1)}, ...), condition=%wide.region_7.9_spmd, body=%wide.region_5.8_spmd.sunk | while | flops 1211891712 | bytes 3197045 | solution.py:29
  166.2 1.6 fusion.44
  168.0 1.6 fusion.44
  169.8 1.6 fusion.44
  171.5 11.0 %collective-permute-done.5 = bf16[1536,768]{1,0:T(8,128)(2,1)} collective-permute-done((bf16[1536,768]{1,0:T(8,128)(2,1)}, bf16[1536,768]{1,0:T(8,128)(2,1)}, u32[]{:S(2)}, u32[]{:S(2)}) %collective-permute-start.5) | collective-permute-done | bytes 2359328 | tf_op jit(solution)/shard_map/ppermute | solution.py:9
  182.4 4.0 %collective-permute-start.8 = (bf16[1536,768]{1,0:T(8,128)(2,1)}, bf16[1536,768]{1,0:T(8,128)(2,1)}, u32[]{:S(2)}, u32[]{:S(2)}) collective-permute-start(bf16[1536,768]{1,0:T(8,128)(2,1)} %collective-permute-done.5), channel_id=1, source_target_pairs={{0,1},{1,2},{2,3},{3,0},{4,5},{5,6},{6,7},{7,4},{8,9},{9,10},{10,1... | collective-permute-start | bytes 7077896 | tf_op jit(solution)/shard_map/ppermute | solution.py:9
  186.4 10.2 %while.41 = (s32[]{:T(128)}, f32[3,512]{1,0:T(4,128)S(1)}, f32[3,512]{1,0:T(4,128)S(1)}, s32[3,512]{1,0:T(4,128)S(1)}, s32[1536]{0:T(1024)S(1)}, /*index=5*/s32[...) while((s32[]{:T(128)}, f32[3,512]{1,0:T(4,128)S(1)}, ...), condition=%wide.region_10.12_spmd, body=%wide.region_8.11_spmd.sunk | while | flops 1211891712 | bytes 3186813 | solution.py:29
  186.4 3.3 %fusion.47 = f32[512]{0:T(512)S(1)} fusion(bf16[1536,768]{1,0:T(8,128)(2,1)} %get-tuple-element.569, s32[512]{0:T(512)S(1)} %bitcast.80, s32[1536]{0:T(1024)S(1)} %get-tuple-element.566, s32[1536]{0:T(1024)S(1)} %get-tuple-element.565, s32[512]{0:T(512)S(1)} %bitcast.81, bf16[3,512,768]{2,1,0:T(8,128)(2,1)S(1)} %get-tuple-element.568, ...), kind=kOutput, calls=%fused_computation.9.clone.1 | convolution fusion | flops 1211891200 | bytes 3168260 | tf_op jit(solution)/shard_map/while/body/eval_jaxpr/dot_general | solution.py:21
  189.8 3.3 %fusion.47 = f32[512]{0:T(512)S(1)} fusion(bf16[1536,768]{1,0:T(8,128)(2,1)} %get-tuple-element.569, s32[512]{0:T(512)S(1)} %bitcast.80, s32[1536]{0:T(1024)S(1)} %get-tuple-element.566, s32[1536]{0:T(1024)S(1)} %get-tuple-element.565, s32[512]{0:T(512)S(1)} %bitcast.81, bf16[3,512,768]{2,1,0:T(8,128)(2,1)S(1)} %get-tuple-element.568, ...), kind=kOutput, calls=%fused_computation.9.clone.1 | convolution fusion | flops 1211891200 | bytes 3168260 | tf_op jit(solution)/shard_map/while/body/eval_jaxpr/dot_general | solution.py:21
  193.3 3.3 %fusion.47 = f32[512]{0:T(512)S(1)} fusion(bf16[1536,768]{1,0:T(8,128)(2,1)} %get-tuple-element.569, s32[512]{0:T(512)S(1)} %bitcast.80, s32[1536]{0:T(1024)S(1)} %get-tuple-element.566, s32[1536]{0:T(1024)S(1)} %get-tuple-element.565, s32[512]{0:T(512)S(1)} %bitcast.81, bf16[3,512,768]{2,1,0:T(8,128)(2,1)S(1)} %get-tuple-element.568, ...), kind=kOutput, calls=%fused_computation.9.clone.1 | convolution fusion | flops 1211891200 | bytes 3168260 | tf_op jit(solution)/shard_map/while/body/eval_jaxpr/dot_general | solution.py:21
  196.6 10.3 %while.42 = (s32[]{:T(128)}, f32[3,512]{1,0:T(4,128)S(1)}, f32[3,512]{1,0:T(4,128)S(1)}, s32[3,512]{1,0:T(4,128)S(1)}, s32[1536]{0:T(1024)}, /*index=5*/s32[1536...) while((s32[]{:T(128)}, f32[3,512]{1,0:T(4,128)S(1)}, ...), condition=%wide.region_13.15_spmd, body=%wide.region_11.14_spmd.sunk | while | flops 1211891712 | bytes 3182717 | solution.py:29
  196.7 3.3 %fusion.50 = f32[512]{0:T(512)S(1)} fusion(bf16[1536,768]{1,0:T(8,128)(2,1)} %get-tuple-element.602, s32[512]{0:T(512)S(1)} %bitcast.82, s32[1536]{0:T(1024)} %get-tuple-element.599, s32[1536]{0:T(1024)} %get-tuple-element.598, s32[512]{0:T(512)S(1)} %bitcast.83, bf16[3,512,768]{2,1,0:T(8,128)(2,1)S(1)} %get-tuple-element.601, s32[]{:T(128)} %get-tuple-element.583), kind=kOutput, calls=%fused_computation.17.clone.1 | convolution fusion | flops 1211891200 | bytes 3164164 | tf_op jit(solution)/shard_map/while/body/eval_jaxpr/dot_general | solution.py:21
  200.1 3.3 %fusion.50 = f32[512]{0:T(512)S(1)} fusion(bf16[1536,768]{1,0:T(8,128)(2,1)} %get-tuple-element.602, s32[512]{0:T(512)S(1)} %bitcast.82, s32[1536]{0:T(1024)} %get-tuple-element.599, s32[1536]{0:T(1024)} %get-tuple-element.598, s32[512]{0:T(512)S(1)} %bitcast.83, bf16[3,512,768]{2,1,0:T(8,128)(2,1)S(1)} %get-tuple-element.601, s32[]{:T(128)} %get-tuple-element.583), kind=kOutput, calls=%fused_computation.17.clone.1 | convolution fusion | flops 1211891200 | bytes 3164164 | tf_op jit(solution)/shard_map/while/body/eval_jaxpr/dot_general | solution.py:21
  203.6 3.3 %fusion.50 = f32[512]{0:T(512)S(1)} fusion(bf16[1536,768]{1,0:T(8,128)(2,1)} %get-tuple-element.602, s32[512]{0:T(512)S(1)} %bitcast.82, s32[1536]{0:T(1024)} %get-tuple-element.599, s32[1536]{0:T(1024)} %get-tuple-element.598, s32[512]{0:T(512)S(1)} %bitcast.83, bf16[3,512,768]{2,1,0:T(8,128)(2,1)S(1)} %get-tuple-element.601, s32[]{:T(128)} %get-tuple-element.583), kind=kOutput, calls=%fused_computation.17.clone.1 | convolution fusion | flops 1211891200 | bytes 3164164 | tf_op jit(solution)/shard_map/while/body/eval_jaxpr/dot_general | solution.py:21
  207.0 5.5 %collective-permute-done.8 = bf16[1536,768]{1,0:T(8,128)(2,1)} collective-permute-done((bf16[1536,768]{1,0:T(8,128)(2,1)}, bf16[1536,768]{1,0:T(8,128)(2,1)}, u32[]{:S(2)}, u32[]{:S(2)}) %collective-permute-start.8) | collective-permute-done | bytes 2359328 | tf_op jit(solution)/shard_map/ppermute | solution.py:9
  212.5 10.2 %while.43 = (s32[]{:T(128)}, f32[3,512]{1,0:T(4,128)S(1)}, f32[3,512]{1,0:T(4,128)S(1)}, s32[3,512]{1,0:T(4,128)S(1)}, s32[1536]{0:T(1024)S(1)}, /*index=5*/s32[...) while((s32[]{:T(128)}, f32[3,512]{1,0:T(4,128)S(1)}, ...), condition=%wide.region_16.18_spmd, body=%wide.region_14.17_spmd.sunk | while | flops 1211891712 | bytes 3186813 | solution.py:29
  212.6 3.3 %fusion.53 = f32[512]{0:T(512)S(1)} fusion(bf16[1536,768]{1,0:T(8,128)(2,1)} %get-tuple-element.635, s32[512]{0:T(512)S(1)} %bitcast.84, s32[1536]{0:T(1024)S(1)} %get-tuple-element.632, s32[1536]{0:T(1024)S(1)} %get-tuple-element.631, s32[512]{0:T(512)S(1)} %bitcast.85, bf16[3,512,768]{2,1,0:T(8,128)(2,1)S(1)} %get-tuple-element.634, ...), kind=kOutput, calls=%fused_computation.25.clone.1 | convolution fusion | flops 1211891200 | bytes 3168260 | tf_op jit(solution)/shard_map/while/body/eval_jaxpr/dot_general | solution.py:21
  216.0 3.3 %fusion.53 = f32[512]{0:T(512)S(1)} fusion(bf16[1536,768]{1,0:T(8,128)(2,1)} %get-tuple-element.635, s32[512]{0:T(512)S(1)} %bitcast.84, s32[1536]{0:T(1024)S(1)} %get-tuple-element.632, s32[1536]{0:T(1024)S(1)} %get-tuple-element.631, s32[512]{0:T(512)S(1)} %bitcast.85, bf16[3,512,768]{2,1,0:T(8,128)(2,1)S(1)} %get-tuple-element.634, ...), kind=kOutput, calls=%fused_computation.25.clone.1 | convolution fusion | flops 1211891200 | bytes 3168260 | tf_op jit(solution)/shard_map/while/body/eval_jaxpr/dot_general | solution.py:21
  219.4 3.3 %fusion.53 = f32[512]{0:T(512)S(1)} fusion(bf16[1536,768]{1,0:T(8,128)(2,1)} %get-tuple-element.635, s32[512]{0:T(512)S(1)} %bitcast.84, s32[1536]{0:T(1024)S(1)} %get-tuple-element.632, s32[1536]{0:T(1024)S(1)} %get-tuple-element.631, s32[512]{0:T(512)S(1)} %bitcast.85, bf16[3,512,768]{2,1,0:T(8,128)(2,1)S(1)} %get-tuple-element.634, ...), kind=kOutput, calls=%fused_computation.25.clone.1 | convolution fusion | flops 1211891200 | bytes 3168260 | tf_op jit(solution)/shard_map/while/body/eval_jaxpr/dot_general | solution.py:21
  222.8 8.4 %gather_fusion.1 = f32[1536]{0:T(1024)S(1)} fusion(f32[1536]{0:T(1024)S(1)} %reshape.200, s32[2048]{0:T(1024)S(1)} %pad_clamp_fusion), kind=kCustom, calls=%fused_computation.4 | custom fusion | bytes 18432 | tf_op jit(solution)/shard_map/jit(_take)/gather | solution.py:93
  231.2 0.7 all_to_all.29
  231.9 10.7 %all-to-all-start.2 = ((s32[128,1,12]{2,1,0:T(1,128)}), s32[128,1,12]{2,1,0:T(1,128)S(1)}, u32[]{:S(2)}, u32[]{:S(2)}) async-start(s32[128,1,12]{2,1,0:T(1,128)} %bitcast.18), calls=%async_computation.2 | async-start | bytes 131072 | tf_op jit(solution)/shard_map/all_to_all | solution.py:103
  242.6 0.7 select_n.88
  243.3 6.2 %all-to-all-done.2 = s32[128,1,12]{2,1,0:T(1,128)S(1)} async-done(((s32[128,1,12]{2,1,0:T(1,128)}), s32[128,1,12]{2,1,0:T(1,128)S(1)}, u32[]{:S(2)}, u32[]{:S(2)}) %all-to-all-start.2) | async-done | bytes 6176 | tf_op jit(solution)/shard_map/all_to_all | solution.py:103
  249.6 6.7 %all-to-all-start.4 = ((f32[128,1,12]{2,1,0:T(1,128)}), f32[128,1,12]{2,1,0:T(1,128)S(1)}, u32[]{:S(2)}, u32[]{:S(2)}) async-start(f32[128,1,12]{2,1,0:T(1,128)} %bitcast.20), calls=%async_computation.4 | async-start | bytes 131072 | tf_op jit(solution)/shard_map/all_to_all | solution.py:96
  256.3 0.7 reduce.21
  257.0 0.1 reshape.195
  257.2 6.1 %all-to-all-done.4 = f32[128,1,12]{2,1,0:T(1,128)S(1)} async-done(((f32[128,1,12]{2,1,0:T(1,128)}), f32[128,1,12]{2,1,0:T(1,128)S(1)}, u32[]{:S(2)}, u32[]{:S(2)}) %all-to-all-start.4) | async-done | bytes 6176 | tf_op jit(solution)/shard_map/all_to_all | solution.py:96
  263.3 0.5 broadcast.139
  263.8 0.8 reduce.22
  264.7 6.7 %scatter_custom_fusion.2 = f32[1536]{0:T(1024)} fusion(s32[1536]{0:T(1024)S(1)} %fusion.21, f32[1536]{0:T(1024)S(1)} %reshape.262, f32[]{:T(128)} %constant.123.clone.1), kind=kCustom, calls=%fused_computation.67 | custom fusion | bytes 6148 | tf_op jit(solution)/shard_map/scatter | solution.py:114
  (79 shorter events, 1.5 us)
Async XLA Ops:
  14.9 20.0 %copy-start = (bf16[1536,768]{1,0:T(8,128)(2,1)S(1)}, bf16[1536,768]{1,0:T(8,128)(2,1)}, u32[]{:S(2)}) copy-start(bf16[1536,768]{1,0:T(8,128)(2,1)} %param.13) | copy-start | bytes 7077892
  24.0 24.0 %all-to-all-start = ((s32[128,1,12]{2,1,0:T(1,128)}), s32[128,1,12]{2,1,0:T(1,128)S(1)}, u32[]{:S(2)}, u32[]{:S(2)}) async-start(s32[128,1,12]{2,1,0:T(1,128)} %bitcast.16), calls=%async_computation | async-start | bytes 131072 | tf_op jit(solution)/shard_map/all_to_all | solution.py:64
  34.9 1.7 copy-start.1
  48.0 50.1 %all-to-all-start.3 = ((bf16[128,12,768]{2,1,0:T(8,128)(2,1)}), bf16[128,12,768]{2,1,0:T(8,128)(2,1)S(1)}, u32[]{:S(2)}, u32[]{:S(2)}) async-start(bf16[128,12,768]{2,1,0:T(8,128)(2,1)} %broadcast_select_fusion), calls=%async_computation.3 | async-start | bytes 6291456 | tf_op jit(solution)/shard_map/all_to_all | solution.py:57
  100.3 18.9 %copy-start.2 = (s32[1,1536]{1,0:T(1,128)S(1)}, s32[1,1536]{1,0:T(1,128)}, u32[]{:S(2)}) copy-start(s32[1,1536]{1,0:T(1,128)} %param.15) | copy-start | bytes 18436
  109.0 47.3 %collective-permute-start.2 = (bf16[1536,768]{1,0:T(8,128)(2,1)S(1)}, bf16[1536,768]{1,0:T(8,128)(2,1)}, u32[]{:S(2)}, u32[]{:S(2)}) collective-permute-start(bf16[1536,768]{1,0:T(8,128)(2,1)S(1)} %scatter_custom_fusion.1), channel_id=1, source_target_pairs={{0,1},{1,2},{2,3},{3,0},{4,5},{5,6},{6,7},{7,4},{8,9},{9,10},{10,1... | collective-permute-start | bytes 7077896 | tf_op jit(solution)/shard_map/ppermute | solution.py:9
  111.1 29.0 %all-to-all-start.1 = ((s32[128,1,12]{2,1,0:T(1,128)}), s32[128,1,12]{2,1,0:T(1,128)S(1)}, u32[]{:S(2)}, u32[]{:S(2)}) async-start(s32[128,1,12]{2,1,0:T(1,128)} %bitcast.17), calls=%async_computation.1 | async-start | bytes 131072 | tf_op jit(solution)/shard_map/all_to_all | solution.py:71
  119.2 34.6 %collective-permute-start = (s32[1536]{0:T(1024)S(1)}, s32[1536]{0:T(1024)S(1)}, u32[]{:S(2)}, u32[]{:S(2)}) collective-permute-start(s32[1536]{0:T(1024)S(1)} %reduce.6), channel_id=1, source_target_pairs={{0,1},{1,2},{2,3},{3,0},{4,5},{5,6},{6,7},{7,4},{8,9},{9,10},{10,1... | collective-permute-start | bytes 18440 | tf_op jit(solution)/shard_map/ppermute | solution.py:9
  147.1 6.8 %collective-permute-start.1 = (s32[1536]{0:T(1024)S(1)}, s32[1536]{0:T(1024)S(1)}, u32[]{:S(2)}, u32[]{:S(2)}) collective-permute-start(s32[1536]{0:T(1024)S(1)} %scatter_custom_fusion), channel_id=1, source_target_pairs={{0,1},{1,2},{2,3},{3,0},{4,5},{5,6},{6,7},{7,4},{8,9},{9,10},{10,1... | collective-permute-start | bytes 18440 | tf_op jit(solution)/shard_map/ppermute | solution.py:9
  153.8 11.0 %collective-permute-start.3 = (s32[1536]{0:T(1024)S(1)}, s32[1536]{0:T(1024)}, u32[]{:S(2)}, u32[]{:S(2)}) collective-permute-start(s32[1536]{0:T(1024)S(1)} %collective-permute-done), channel_id=1, source_target_pairs={{0,1},{1,2},{2,3},{3,0},{4,5},{5,6},{6,7},{7,4},{8,9},{9,10},{10,1... | collective-permute-start | bytes 18440 | tf_op jit(solution)/shard_map/ppermute | solution.py:9
  153.9 12.2 %collective-permute-start.4 = (s32[1536]{0:T(1024)S(1)}, s32[1536]{0:T(1024)}, u32[]{:S(2)}, u32[]{:S(2)}) collective-permute-start(s32[1536]{0:T(1024)S(1)} %collective-permute-done.1), channel_id=1, source_target_pairs={{0,1},{1,2},{2,3},{3,0},{4,5},{5,6},{6,7},{7,4},{8,9},{9,10},{10,1... | collective-permute-start | bytes 18440 | tf_op jit(solution)/shard_map/ppermute | solution.py:9
  156.3 26.2 %collective-permute-start.5 = (bf16[1536,768]{1,0:T(8,128)(2,1)}, bf16[1536,768]{1,0:T(8,128)(2,1)}, u32[]{:S(2)}, u32[]{:S(2)}) collective-permute-start(bf16[1536,768]{1,0:T(8,128)(2,1)} %collective-permute-done.2), channel_id=1, source_target_pairs={{0,1},{1,2},{2,3},{3,0},{4,5},{5,6},{6,7},{7,4},{8,9},{9,10},{10,1... | collective-permute-start | bytes 7077896 | tf_op jit(solution)/shard_map/ppermute | solution.py:9
  164.8 42.2 %collective-permute-start.6 = (s32[1536]{0:T(1024)}, s32[1536]{0:T(1024)S(1)}, u32[]{:S(2)}, u32[]{:S(2)}) collective-permute-start(s32[1536]{0:T(1024)} %collective-permute-done.3), channel_id=1, source_target_pairs={{0,1},{1,2},{2,3},{3,0},{4,5},{5,6},{6,7},{7,4},{8,9},{9,10},{10,1... | collective-permute-start | bytes 18440 | tf_op jit(solution)/shard_map/ppermute | solution.py:9
  166.1 40.9 %collective-permute-start.7 = (s32[1536]{0:T(1024)}, s32[1536]{0:T(1024)S(1)}, u32[]{:S(2)}, u32[]{:S(2)}) collective-permute-start(s32[1536]{0:T(1024)} %collective-permute-done.4), channel_id=1, source_target_pairs={{0,1},{1,2},{2,3},{3,0},{4,5},{5,6},{6,7},{7,4},{8,9},{9,10},{10,1... | collective-permute-start | bytes 18440 | tf_op jit(solution)/shard_map/ppermute | solution.py:9
  182.4 30.1 %collective-permute-start.8 = (bf16[1536,768]{1,0:T(8,128)(2,1)}, bf16[1536,768]{1,0:T(8,128)(2,1)}, u32[]{:S(2)}, u32[]{:S(2)}) collective-permute-start(bf16[1536,768]{1,0:T(8,128)(2,1)} %collective-permute-done.5), channel_id=1, source_target_pairs={{0,1},{1,2},{2,3},{3,0},{4,5},{5,6},{6,7},{7,4},{8,9},{9,10},{10,1... | collective-permute-start | bytes 7077896 | tf_op jit(solution)/shard_map/ppermute | solution.py:9
  231.9 17.6 %all-to-all-start.2 = ((s32[128,1,12]{2,1,0:T(1,128)}), s32[128,1,12]{2,1,0:T(1,128)S(1)}, u32[]{:S(2)}, u32[]{:S(2)}) async-start(s32[128,1,12]{2,1,0:T(1,128)} %bitcast.18), calls=%async_computation.2 | async-start | bytes 131072 | tf_op jit(solution)/shard_map/all_to_all | solution.py:103
  249.6 13.7 %all-to-all-start.4 = ((f32[128,1,12]{2,1,0:T(1,128)}), f32[128,1,12]{2,1,0:T(1,128)S(1)}, u32[]{:S(2)}, u32[]{:S(2)}) async-start(f32[128,1,12]{2,1,0:T(1,128)} %bitcast.20), calls=%async_computation.4 | async-start | bytes 131072 | tf_op jit(solution)/shard_map/all_to_all | solution.py:96
where the time goes:
time: 276 us; the launch traced here: 271 us
  waiting for transfers between devices  86.4 us (31%)
  local copies, waits for them, and re-layouts  72.7 us (26%)
  starting transfers between devices  59.2 us (21%)
  matrix products  34.8 us (13%)
  other arithmetic  17.7 us (6%)
    all_to_all x1, waiting for transfers between devices, on_device(): lax.all_to_all(sent_unit.reshape(device_count, pair_rows, width), ('grp',...  38.9 us
    dot_general x12, matrix products, one_block(): lax.dot_general(unit_part, unit_other, (((1,), (1,)), ((), ())), preferre...  34.8 us
    all_to_all x1, waiting for transfers between devices, on_device(): lax.all_to_all(sent_index.reshape(device_count, pair_rows), ('grp', 'blk'...  18.5 us
    ppermute x9, waiting for transfers between devices, passed_along(): lax.ppermute(shard, axis, [(i, (i + by) % size) for i in range(size)])  16.5 us
    ppermute x9, starting transfers between devices, passed_along(): lax.ppermute(shard, axis, [(i, (i + by) % size) for i in range(size)])  13.3 us
    all_to_all x1, starting transfers between devices, on_device(): lax.all_to_all(sent_slot.reshape(device_count, pair_rows), ('grp', 'blk')...  10.7 us
    all_to_all x1, starting transfers between devices, on_device(): lax.all_to_all(home_pos.reshape(device_count, pair_rows), ('grp', 'blk'),...  10.7 us
    all_to_all x1, starting transfers between devices, on_device(): lax.all_to_all(sent_unit.reshape(device_count, pair_rows, width), ('grp',...  9.76 us
  transfers between devices with their start and end apart: 14, of which 6 were waited for; matrix products, arithmetic and copies ran while one was open for 23% of the time, Pallas kernels for 0%

commit v1 on v0

v1 whole, which is shorter than its diff:
```python
import functools

import jax
import jax.numpy as jnp
from jax import lax
from jax.experimental import pallas as pl
from jax.experimental.pallas import tpu as pltpu
from jax.sharding import PartitionSpec as P

MESH = pl.DeviceIdType.MESH
F32, BF16, I32 = jnp.float32, jnp.bfloat16, jnp.int32
SLAB = 40
USED = 36
WINDOWS = 8
CHUNK = 16 * SLAB


def dot(a, b):
    return lax.dot_general(a, b, (((1,), (0,)), ((), ())), preferred_element_type=F32)


def dot_t(a, b):
    return lax.dot_general(a, b, (((1,), (1,)), ((), ())), preferred_element_type=F32)


def iota(shape, dim):
    return lax.broadcasted_iota(I32, shape, dim)


def quotient(value, by):
    return jnp.floor((value + 0.5) * (1.0 / by))


def thirds(value):
    first = value.astype(BF16)
    rest = value - first.astype(F32)
    second = rest.astype(BF16)
    return first, second, (rest - second.astype(F32)).astype(BF16)


def window_shift(w):
    return w // 2, w % 2


def chip_of(u, v, e, x):
    return x, (u + x) % 4, (v + 2 * e + x) % 4


def device_of(x, y, z, core):
    return (y % 2) * 16 + z * 4 + x, (y // 2) * 2 + core


def kernel(
    emb_ref, route_ref, cluster_ref, out_ref,
    unit, send, rows, table, picks, ranks, meta, count, counts, spread, key_col, key_row, cl_col, cl_row, best, gone, back,
    send_sem, recv_sem, pass_sem, pass_send_sem, count_sem, count_send_sem, back_sem, back_send_sem,
):
    row_count, width = emb_ref.shape
    grp, blk = lax.axis_index("grp"), lax.axis_index("blk")
    me = grp * 4 + blk
    y_lo, z0, x0 = grp // 16, (grp // 4) % 4, grp % 4
    y0, core = (blk // 2) * 2 + y_lo, blk % 2
    u0, v0, e0 = (y0 - x0 + 4) % 4, (z0 - x0 + 4) % 2, ((z0 - x0 + 4) % 4) // 2
    sibling = (grp, blk + 1 - 2 * core)

    barrier = pltpu.get_barrier_semaphore()

    def greet(i, carry):
        other = (me + 1 + i) % 128
        pl.semaphore_signal(barrier, inc=1, device_id=(other // 4, other % 4), device_id_type=MESH)
        return carry

    lax.fori_loop(0, 127, greet, 0)

    values = emb_ref[...].astype(F32)
    unit[...] = (values * lax.rsqrt(jnp.sum(values * values, axis=1, keepdims=True) + 1e-06)).astype(BF16)

    route = route_ref[...].astype(F32)
    family = quotient(route, 6144)
    slot = route - family * 6144
    block = quotient(slot, 1536)
    slot_hi = quotient(slot, 48)
    slot_lo = slot - slot_hi * 48
    family_int = family.astype(I32)
    fam_y, fam_z, fam_x = family_int >> 4, (family_int >> 2) & 3, family_int & 3

    def order_number(y):
        dx, dy, dz = (fam_x - x0) & 3, (y - y0) & 3, (fam_z - z0) & 3
        du, dzx = (dy - dx) & 3, (dz - dx) & 3
        return (du * 2 + (dzx & 1)) * 8 + (dzx >> 1) * 4 + dx

    pick_a = jnp.where(block < 2.5, order_number(fam_y), -1)
    pick_b = jnp.where(block > 0.5, order_number(fam_y + 2), -1)
    slab_iota = iota((64, row_count), 0)
    hot_a = (slab_iota == pick_a).astype(F32)
    hot_b = (slab_iota == pick_b).astype(F32)
    hot = (hot_a + hot_b).astype(BF16)
    earlier = (iota((256, 256), 0) < iota((256, 256), 1)).astype(F32).astype(BF16)
    before = jnp.zeros((64, 1), F32)
    prefix = []
    for k in range(row_count // 256):
        part = hot[:, k * 256:(k + 1) * 256]
        prefix.append(dot(part, earlier) + before)
        before = before + jnp.sum(part.astype(F32), axis=1, keepdims=True)
    prefix = jnp.concatenate(prefix, axis=1)
    rank_a = jnp.sum(hot_a * prefix, axis=0, keepdims=True).astype(I32)
    rank_b = jnp.sum(hot_b * prefix, axis=0, keepdims=True).astype(I32)
    picks[0:1, :], picks[1:2, :] = pick_a, pick_b
    ranks[0:1, :], ranks[1:2, :] = rank_a, rank_b
    lane_iota = iota((128, row_count), 0)
    hi = jnp.zeros((64, 128), F32)
    lo = jnp.zeros((64, 128), F32)
    for hot_one, rank in ((hot_a, rank_a), (hot_b, rank_b)):
        chosen = lane_iota == rank
        hi = hi + dot_t(hot_one.astype(BF16), jnp.where(chosen, slot_hi, 0.0).astype(BF16))
        lo = lo + dot_t(hot_one.astype(BF16), jnp.where(chosen, slot_lo, 0.0).astype(BF16))
    meta[0:64, :] = hi.astype(BF16)
    meta[64:128, :] = lo.astype(BF16)

    cluster = cluster_ref[...]
    which = iota((8, 128), 0)
    tally = jnp.zeros((8, 128), F32)
    for k in range(1, 4):
        below = jnp.sum((cluster < k).astype(F32), axis=1, keepdims=True)
        tally = jnp.where(which == k, below, tally)
    count[...] = tally

    pl.semaphore_wait(barrier, 127)

    def count_copy(step):
        return pltpu.make_async_remote_copy(
            src_ref=count, dst_ref=counts.at[step], send_sem=count_send_sem.at[step], recv_sem=count_sem.at[step],
            device_id=(grp, (blk + 1 + step) % 4), device_id_type=MESH,
        )

    for step in range(3):
        count_copy(step).start()

    target_a = jnp.where(pick_a >= 0, pick_a * SLAB + rank_a, -1)
    target_b = jnp.where(pick_b >= 0, pick_b * SLAB + rank_b, -1)
    picks[2:3, :], picks[3:4, :] = target_a, target_b
    home_row = ((v0 * 4 + u0) * 16 + (e0 * 4 + x0) * 2 + core) * (SLAB // 8)
    p_col = iota((8 * SLAB, 128), 0).astype(F32)
    p_slab = quotient(p_col, SLAB)
    p_in = (p_col - p_slab * SLAB).astype(I32)
    p_slab = p_slab.astype(I32)
    p_lane = iota((8 * SLAB, 128), 1)

    def make_window(w, carry):
        p_iota = iota((8 * SLAB, row_count), 0) + w * (8 * SLAB)
        one_hot = ((p_iota == picks[2:3, :]) | (p_iota == picks[3:4, :])).astype(F32).astype(BF16)
        body = dot(one_hot, unit[...])
        slab_no = p_slab + w * 8
        info_hot = (((p_in == USED) & (p_lane == slab_no)) | ((p_in == USED + 1) & (p_lane == slab_no + 64))).astype(F32).astype(BF16)
        info = dot(info_hot, meta[...])
        base = w * SLAB
        body = jnp.concatenate([body[:, 0:128] + info, body[:, 128:width]], axis=1).astype(BF16)
        send[pl.ds(base, SLAB)] = body.reshape(SLAB, 8, width)
        du, dv = window_shift(w)

        def send_one(k, inner):
            dx, dy, dz = chip_of(du, dv, k // 4, k % 4)
            to = device_of((x0 + dx) % 4, (y0 + dy) % 4, (z0 + dz) % 4, v0)
            source = send.at[pl.ds((w * 8 + k) * (SLAB // 8), SLAB // 8)]
            here = (to[0] * 4 + to[1]) == me

            @pl.when(jnp.logical_not(here))
            def _():
                pltpu.make_async_remote_copy(
                    src_ref=source, dst_ref=rows.at[pl.ds(home_row, SLAB // 8)], send_sem=send_sem, recv_sem=recv_sem.at[w],
                    device_id=to, device_id_type=MESH,
                ).start()

            @pl.when(here)
            def _():
                pltpu.make_async_copy(source, rows.at[pl.ds(home_row, SLAB // 8)], recv_sem.at[w]).start()

            return inner

        lax.fori_loop(0, 8, send_one, 0)
        return carry

    lax.fori_loop(0, WINDOWS, make_window, 0)

    p = iota((CHUNK, 128), 0).astype(F32)
    slab_of = quotient(p, SLAB)
    in_slab = p - slab_of * SLAB
    diagonal = ((iota((CHUNK, 128), 1).astype(F32) == in_slab) & (in_slab < USED)).astype(F32)
    other = iota((CHUNK, CHUNK), 1).astype(F32)
    p_wide = iota((CHUNK, CHUNK), 0).astype(F32)
    first = quotient(p_wide, SLAB) * SLAB
    spread[...] = jnp.where(other == first + USED, 48.0, jnp.where(other == first + (USED + 1), 1.0, 0.0)).astype(BF16)

    def data_key(slab_no, inside, u, v):
        sx, se, sc = (slab_no >> 1) & 3, slab_no >> 3, slab_no & 1
        sy, sz = (u + sx) & 3, (v + 2 * se + sx) & 3
        source = ((sy & 1) * 16 + sz * 4 + sx) * 4 + (sy >> 1) * 2 + sc
        return source * SLAB + inside

    slab_col, in_col = slab_of.astype(I32), in_slab.astype(I32)
    q = iota((8, CHUNK), 1).astype(F32)
    slab_row = quotient(q, SLAB)
    in_row = (q - slab_row * SLAB).astype(I32)
    slab_row = slab_row.astype(I32)

    def make_keys(k, carry):
        key_col[k] = data_key(slab_col, in_col, k % 4, k // 4)
        key_row[k] = data_key(slab_row, in_row, k % 4, k // 4)
        return carry

    lax.fori_loop(0, WINDOWS, make_keys, 0)
    best[...] = jnp.full(best.shape, -1.0, F32)

    total = count[...]
    for step in range(3):
        count_copy(step).wait()
        total = total + counts[step]
    ends = [total[k:k + 1, :] for k in range(1, 4)]
    ones_col = jnp.ones((128, 128), BF16)
    ones_row = jnp.ones((8, 128), BF16)

    def chunk_of(w):
        du, dv = window_shift(w)
        u, v = (u0 - du + 4) % 4, (v0 - dv + 2) % 2
        return v * 4 + u, v

    def pass_copy(w, chunk):
        part = rows.at[pl.ds(chunk * (CHUNK // 8), CHUNK // 8)]
        return pltpu.make_async_remote_copy(
            src_ref=part, dst_ref=part, send_sem=pass_send_sem.at[w], recv_sem=pass_sem.at[w],
            device_id=sibling, device_id_type=MESH,
        )

    def fold(mine, others):
        x_mine = table[mine]
        x_other = table[others]
        scores = dot_t(x_other, x_mine)
        wide = lambda a: jnp.concatenate([a] * (CHUNK // 128), axis=1)
        same = wide(cl_col[others]) == cl_row[mine][0:1, :]
        prior = wide(key_col[others]) < key_row[mine][0:1, :]
        held = jnp.where(same & prior, scores, -1.0).reshape(CHUNK // 8, 8, CHUNK)
        u = mine % 4
        best[u] = jnp.maximum(best[u], jnp.max(held, axis=0))

    def take_window(w, carry):
        chunk, v = chunk_of(w)
        part = rows.at[pl.ds(chunk * (CHUNK // 8), CHUNK // 8)]

        @pl.when(v == core)
        def _():
            pltpu.make_async_copy(part, part, recv_sem.at[w]).wait()
            pass_copy(w, chunk).start()

        @pl.when(v != core)
        def _():
            pltpu.make_async_copy(part, part, pass_sem.at[w]).wait()

        table[chunk] = rows[pl.ds(chunk * (CHUNK // 8), CHUNK // 8)].reshape(CHUNK, width)
        slots = dot(spread[...], table[chunk][:, 0:128])
        number = 1.0
        for end in ends:
            number = number + (slots >= end).astype(F32)
        number = (number * diagonal).astype(BF16)
        cl_col[chunk] = dot(number, ones_col)
        cl_row[chunk] = dot_t(ones_row, number)

        def with_earlier(k, inner):
            chunk_k, v_k = chunk_of(k)

            @pl.when(v == core)
            def _():
                fold(chunk, chunk_k)

            @pl.when((v_k == core) & (k < w))
            def _():
                fold(chunk_k, chunk)

            return inner

        lax.fori_loop(0, w + 1, with_earlier, 0)
        return carry

    lax.fori_loop(0, WINDOWS, take_window, 0)

    slab_lane = quotient(iota((16, CHUNK), 1).astype(F32), SLAB)
    own_slab = slab_lane == iota((16, CHUNK), 0).astype(F32)
    fold_lanes = (diagonal > 0.5).astype(F32).astype(BF16)

    def give_back(u, carry):
        row = jnp.max(best[u], axis=0, keepdims=True)
        picked = jnp.where(own_slab, row, 0.0)
        table = sum(dot(piece, fold_lanes) for piece in thirds(picked))
        gone[pl.ds(pl.multiple_of(u * 16, 16), 16), :] = table

        def one(k, inner):
            sx, sy, sz = chip_of(u, core, k // 8, (k // 2) % 4)
            to = device_of(sx, sy, sz, k % 2)
            dx, dy, dz = (x0 - sx + 4) % 4, (y0 - sy + 4) % 4, (z0 - sz + 4) % 4
            du, dzx = (dy - dx + 4) % 4, (dz - dx + 4) % 4
            number = (du * 2 + dzx % 2) * 8 + (dzx // 2) * 4 + dx
            here = (to[0] * 4 + to[1]) == me

            @pl.when(jnp.logical_not(here))
            def _():
                pltpu.make_async_remote_copy(
                    src_ref=gone.at[pl.ds(u * 16 + k, 1)], dst_ref=back.at[pl.ds(number, 1)], send_sem=back_send_sem, recv_sem=back_sem,
                    device_id=to, device_id_type=MESH,
                ).start()

            @pl.when(here)
            def _():
                pltpu.make_async_copy(gone.at[pl.ds(u * 16 + k, 1)], back.at[pl.ds(number, 1)], back_sem).start()

            return inner

        lax.fori_loop(0, 16, one, 0)
        return carry

    lax.fori_loop(0, 4, give_back, 0)

    mine_too = v0 == core

    @pl.when(mine_too)
    def _():
        pltpu.make_async_copy(send.at[pl.ds(0, 63 * (SLAB // 8))], send.at[pl.ds(0, 63 * (SLAB // 8))], send_sem).wait()

    @pl.when(jnp.logical_not(mine_too))
    def _():
        pltpu.make_async_copy(send, send, send_sem).wait()

    def pass_sent(w, carry):
        chunk, v = chunk_of(w)

        @pl.when(v == core)
        def _():
            pass_copy(w, chunk).wait_send()

        return carry

    lax.fori_loop(0, WINDOWS, pass_sent, 0)

    pltpu.make_async_copy(back, back, back_sem).wait()
    result = jnp.full((1, row_count), -1.0, F32)
    got = jnp.concatenate([back[...], jnp.zeros((64, 128), F32)], axis=0).T
    pieces = thirds(got[:, 0:64])
    for k in range(2):
        hot_one = (slab_iota == picks[k:k + 1, :]).astype(F32).astype(BF16)
        table = sum(dot(piece, hot_one) for piece in pieces)
        mark = (lane_iota == ranks[k:k + 1, :]) & (picks[k:k + 1, :] >= 0)
        result = jnp.maximum(result, jnp.max(jnp.where(mark, table, -1.0), axis=0, keepdims=True))
    out_ref[...] = result

    @pl.when(v0 == core)
    def _():
        pltpu.make_async_copy(gone.at[pl.ds(0, 63)], gone.at[pl.ds(0, 63)], back_send_sem).wait()

    @pl.when(v0 != core)
    def _():
        pltpu.make_async_copy(gone, gone, back_send_sem).wait()


def on_device(embeddings, route, cluster):
    row_count, width = embeddings.shape
    vmem = pl.BlockSpec(memory_space=pltpu.VMEM)
    scores = pl.pallas_call(
        kernel,
        out_shape=jax.ShapeDtypeStruct((1, row_count), F32),
        in_specs=[vmem] * 3,
        out_specs=vmem,
        scratch_shapes=[
            pltpu.VMEM((row_count, width), BF16),
            pltpu.VMEM((8 * SLAB, 8, width), BF16),
            pltpu.VMEM((WINDOWS * CHUNK // 8, 8, width), BF16),
            pltpu.VMEM((WINDOWS, CHUNK, width), BF16),
            pltpu.VMEM((8, row_count), I32),
            pltpu.VMEM((8, row_count), I32),
            pltpu.VMEM((128, 128), BF16),
            pltpu.VMEM((8, 128), F32),
            pltpu.VMEM((3, 8, 128), F32),
            pltpu.VMEM((CHUNK, CHUNK), BF16),
            pltpu.VMEM((WINDOWS, CHUNK, 128), I32),
            pltpu.VMEM((WINDOWS, 8, CHUNK), I32),
            pltpu.VMEM((WINDOWS, CHUNK, 128), F32),
            pltpu.VMEM((WINDOWS, 8, CHUNK), F32),
            pltpu.VMEM((4, 8, CHUNK), F32),
            pltpu.VMEM((64, 128), F32),
            pltpu.VMEM((64, 128), F32),
            pltpu.SemaphoreType.DMA,
            pltpu.SemaphoreType.DMA((WINDOWS,)),
            pltpu.SemaphoreType.DMA((WINDOWS,)),
            pltpu.SemaphoreType.DMA((WINDOWS,)),
            pltpu.SemaphoreType.DMA((3,)),
            pltpu.SemaphoreType.DMA((3,)),
            pltpu.SemaphoreType.DMA,
            pltpu.SemaphoreType.DMA,
        ],
        compiler_params=pltpu.CompilerParams(collective_id=0, has_side_effects=True, vmem_limit_bytes=56 * 1024 * 1024),
    )(embeddings, route.reshape(1, row_count), cluster)
    return scores.reshape(row_count)


def solution(mesh):
    in_specs = (P(("grp", "blk"), None), P(("grp", "blk")), P("grp", "blk"))
    return jax.shard_map(on_device, mesh=mesh, in_specs=in_specs, out_specs=P(("grp", "blk")), check_vma=False)
```

time: 276 us -> 101 us (0.37); the launches traced: 271 us -> 99.6 us
  Pallas kernels: 0 us -> 97 us
  waiting for transfers between devices: 86.4 us -> 0 us
  local copies, waits for them, and re-layouts: 72.7 us -> 1.29 us
  starting transfers between devices: 59.2 us -> 0 us
  matrix products: 34.8 us -> 0 us
  other arithmetic: 17.7 us -> 1.31 us
    pallas_call x0 -> x1, Pallas kernels: none -> 97 us  [on_device(): pl.pallas_call(kernel, out_shape=jax.ShapeDtypeStruct((1, row_count), F32...]
    all_to_all x5 -> x0, waiting for transfers between devices: 69.8 us -> none  [the longest x1 38.9 us: on_device(): lax.all_to_all(sent_unit.reshape(device_count, pair_rows, width), ('grp',...]
    all_to_all x5 -> x0, starting transfers between devices: 45.9 us -> none  [the longest x1 10.7 us: on_device(): lax.all_to_all(sent_slot.reshape(device_count, pair_rows), ('grp', 'blk')...]
    gather x6 -> x0, local copies, waits for them, and re-layouts: 42.7 us -> none  [the longest x2 9.1 us: on_device(): sent_unit = jnp.take(unit_rows, ordering, axis=0)]
    dot_general x12 -> x0, matrix products: 34.8 us -> none  [one_block(): lax.dot_general(unit_part, unit_other, (((1,), (1,)), ((), ())), preferre...]
    scatter x3 -> x0, local copies, waits for them, and re-layouts: 21.7 us -> none  [the longest x1 8.72 us: on_device(): jnp.zeros((row_count, width), jnp.bfloat16).at[slot_pos]]
    ppermute x9 -> x0, waiting for transfers between devices: 16.5 us -> none  [passed_along(): lax.ppermute(shard, axis, [(i, (i + by) % size) for i in range(size)])]
    ppermute x9 -> x0, starting transfers between devices: 13.3 us -> none  [passed_along(): lax.ppermute(shard, axis, [(i, (i + by) % size) for i in range(size)])]
  transfers between devices with their start and end apart: 14 -> 0, of which waited for: 6 -> 0; matrix products, arithmetic and copies ran while one was open for 23% -> 0% of each run, Pallas kernels for 0% -> 0%
where the time goes in v1:
time: 101 us; the launch traced here: 99.6 us
  Pallas kernels  97 us (96%)
  other arithmetic  1.31 us (1%)
  local copies, waits for them, and re-layouts  1.29 us (1%)
    pallas_call x1, Pallas kernels, on_device(): pl.pallas_call(kernel, out_shape=jax.ShapeDtypeStruct((1, row_count), F32...  97 us

profile of v1, /device:TPU:13, one launch (start us, length us, event | category | flops | bytes accessed | tf_op | source)
XLA Modules:
  0.0 99.6 jit_solution(187136465741298909)
XLA Ops:
  0.0 1.3 %reshape.6.route_ref = s32[1,1536]{1,0:T(1,128)} reshape(s32[1536]{0:T(1024)} %param.4) | data formatting | bytes 12288 | tf_op jit(solution)/shard_map/reshape | solution.py:398
  1.3 97.0 %shard_map.37 = f32[1,1536]{1,0:T(1,128)} custom-call(bf16[1536,768]{1,0:T(8,128)(2,1)} %emb_ref.1, s32[1,1536]{1,0:T(1,128)} %reshape.6.route_ref, s32[1,1536]{1,0:T(1,128)} %cluster_ref.1), custom_call_target="tpu_custom_call" | custom-call | tf_op jit(solution)/shard_map/pallas_call | solution.py:365
  98.3 1.3 %reduce = f32[1536]{0:T(1024)} reduce(f32[1,1536]{1,0:T(1,128)} %shard_map.37, f32[]{:T(128)} %constant.1), dimensions={0}, to_apply=%pallas_call.3.reduce_sub_computation | reduce | bytes 12292 | tf_op jit(solution)/shard_map/pallas_call | solution.py:365

commit v2 on v1

--- a/solution.py
+++ b/solution.py
@@ -39,7 +39,7 @@
 
 
 def window_shift(w):
-    return w // 2, w % 2
+    return (7 - w) // 2, (7 - w) % 2
 
 
 def chip_of(u, v, e, x):
@@ -52,7 +52,7 @@
 
 def kernel(
     emb_ref, route_ref, cluster_ref, out_ref,
-    unit, send, rows, table, picks, ranks, meta, count, counts, spread, key_col, key_row, cl_col, cl_row, best, gone, back,
+    unit, send, rows, table, picks, ranks, meta, count, counts, spread, key_col, key_row, cl_col, cl_row, best, best_t, gone, back,
     send_sem, recv_sem, pass_sem, pass_send_sem, count_sem, count_send_sem, back_sem, back_send_sem,
 ):
     row_count, width = emb_ref.shape
@@ -75,7 +75,7 @@
     values = emb_ref[...].astype(F32)
     unit[...] = (values * lax.rsqrt(jnp.sum(values * values, axis=1, keepdims=True) + 1e-06)).astype(BF16)
 
-    route = route_ref[...].astype(F32)
+    route = jnp.concatenate([route_ref[k:k + 1, :] for k in range(row_count // 128)], axis=1).astype(F32)
     family = quotient(route, 6144)
     slot = route - family * 6144
     block = quotient(slot, 1536)
@@ -87,7 +87,7 @@
     def order_number(y):
         dx, dy, dz = (fam_x - x0) & 3, (y - y0) & 3, (fam_z - z0) & 3
         du, dzx = (dy - dx) & 3, (dz - dx) & 3
-        return (du * 2 + (dzx & 1)) * 8 + (dzx >> 1) * 4 + dx
+        return (7 - du * 2 - (dzx & 1)) * 8 + (1 - (dzx >> 1)) * 4 + 3 - dx
 
     pick_a = jnp.where(block < 2.5, order_number(fam_y), -1)
     pick_b = jnp.where(block > 0.5, order_number(fam_y + 2), -1)
@@ -159,7 +159,7 @@
         du, dv = window_shift(w)
 
         def send_one(k, inner):
-            dx, dy, dz = chip_of(du, dv, k // 4, k % 4)
+            dx, dy, dz = chip_of(du, dv, 1 - k // 4, 3 - k % 4)
             to = device_of((x0 + dx) % 4, (y0 + dy) % 4, (z0 + dz) % 4, v0)
             source = send.at[pl.ds((w * 8 + k) * (SLAB // 8), SLAB // 8)]
             here = (to[0] * 4 + to[1]) == me
@@ -210,6 +210,7 @@
 
     lax.fori_loop(0, WINDOWS, make_keys, 0)
     best[...] = jnp.full(best.shape, -1.0, F32)
+    best_t[...] = jnp.full(best_t.shape, -1.0, F32)
 
     total = count[...]
     for step in range(3):
@@ -231,7 +232,7 @@
             device_id=sibling, device_id_type=MESH,
         )
 
-    def fold(mine, others):
+    def fold(mine, others, both=False):
         x_mine = table[mine]
         x_other = table[others]
         scores = dot_t(x_other, x_mine)
@@ -241,6 +242,13 @@
         held = jnp.where(same & prior, scores, -1.0).reshape(CHUNK // 8, 8, CHUNK)
         u = mine % 4
         best[u] = jnp.maximum(best[u], jnp.max(held, axis=0))
+        if both:
+            later = jnp.where(same & jnp.logical_not(prior), scores, -1.0)
+            most = later[:, 0:128]
+            for k in range(1, CHUNK // 128):
+                most = jnp.maximum(most, later[:, k * 128:(k + 1) * 128])
+            t = others % 4
+            best_t[t] = jnp.maximum(best_t[t], most)
 
     def take_window(w, carry):
         chunk, v = chunk_of(w)
@@ -267,11 +275,15 @@
         def with_earlier(k, inner):
             chunk_k, v_k = chunk_of(k)
 
-            @pl.when(v == core)
+            @pl.when((v == core) & ((v_k != core) | (k == w)))
             def _():
                 fold(chunk, chunk_k)
 
-            @pl.when((v_k == core) & (k < w))
+            @pl.when((v == core) & (v_k == core) & (k < w))
+            def _():
+                fold(chunk, chunk_k, both=True)
+
+            @pl.when((v != core) & (v_k == core))
             def _():
                 fold(chunk_k, chunk)
 
@@ -284,20 +296,23 @@
 
     slab_lane = quotient(iota((16, CHUNK), 1).astype(F32), SLAB)
     own_slab = slab_lane == iota((16, CHUNK), 0).astype(F32)
+    as_slabs = own_slab.astype(F32).astype(BF16)
     fold_lanes = (diagonal > 0.5).astype(F32).astype(BF16)
 
     def give_back(u, carry):
         row = jnp.max(best[u], axis=0, keepdims=True)
         picked = jnp.where(own_slab, row, 0.0)
         table = sum(dot(piece, fold_lanes) for piece in thirds(picked))
-        gone[pl.ds(pl.multiple_of(u * 16, 16), 16), :] = table
+        listed = jnp.where(diagonal > 0.5, jnp.max(best_t[u], axis=1, keepdims=True), 0.0)
+        table_t = sum(dot(as_slabs, piece) for piece in thirds(listed))
+        gone[pl.ds(pl.multiple_of(u * 16, 16), 16), :] = jnp.maximum(table, table_t)
 
         def one(k, inner):
             sx, sy, sz = chip_of(u, core, k // 8, (k // 2) % 4)
             to = device_of(sx, sy, sz, k % 2)
             dx, dy, dz = (x0 - sx + 4) % 4, (y0 - sy + 4) % 4, (z0 - sz + 4) % 4
             du, dzx = (dy - dx + 4) % 4, (dz - dx + 4) % 4
-            number = (du * 2 + dzx % 2) * 8 + (dzx // 2) * 4 + dx
+            number = (7 - du * 2 - dzx % 2) * 8 + (1 - dzx // 2) * 4 + 3 - dx
             here = (to[0] * 4 + to[1]) == me
 
             @pl.when(jnp.logical_not(here))
@@ -348,7 +363,8 @@
         table = sum(dot(piece, hot_one) for piece in pieces)
         mark = (lane_iota == ranks[k:k + 1, :]) & (picks[k:k + 1, :] >= 0)
         result = jnp.maximum(result, jnp.max(jnp.where(mark, table, -1.0), axis=0, keepdims=True))
-    out_ref[...] = result
+    for k in range(row_count // 128):
+        out_ref[k:k + 1, :] = result[:, k * 128:(k + 1) * 128]
 
     @pl.when(v0 == core)
     def _():
@@ -364,7 +380,7 @@
     vmem = pl.BlockSpec(memory_space=pltpu.VMEM)
     scores = pl.pallas_call(
         kernel,
-        out_shape=jax.ShapeDtypeStruct((1, row_count), F32),
+        out_shape=jax.ShapeDtypeStruct((row_count // 128, 128), F32),
         in_specs=[vmem] * 3,
         out_specs=vmem,
         scratch_shapes=[
@@ -383,6 +399,7 @@
             pltpu.VMEM((WINDOWS, CHUNK, 128), F32),
             pltpu.VMEM((WINDOWS, 8, CHUNK), F32),
             pltpu.VMEM((4, 8, CHUNK), F32),
+            pltpu.VMEM((4, CHUNK, 128), F32),
             pltpu.VMEM((64, 128), F32),
             pltpu.VMEM((64, 128), F32),
             pltpu.SemaphoreType.DMA,
@@ -395,7 +412,7 @@
             pltpu.SemaphoreType.DMA,
         ],
         compiler_params=pltpu.CompilerParams(collective_id=0, has_side_effects=True, vmem_limit_bytes=56 * 1024 * 1024),
-    )(embeddings, route.reshape(1, row_count), cluster)
+    )(embeddings, route.reshape(row_count // 128, 128), cluster)
     return scores.reshape(row_count)
 
 

time: 101 us -> 95.1 us (0.942); the launches traced: 99.6 us -> 94.9 us
  Pallas kernels: 97 us -> 93.6 us
  other arithmetic: 1.31 us -> 0 us
    pallas_call x1, Pallas kernels: 97 us -> 93.6 us  [on_device(): pl.pallas_call(kernel, out_shape=jax.ShapeDtypeStruct((row_count // 128,...]
    pallas_call x1 -> x0, other arithmetic: 1.31 us -> none  [on_device(): pl.pallas_call(kernel, out_shape=jax.ShapeDtypeStruct((1, row_count), F32...]
    unnamed x0 -> x1, local copies, waits for them, and re-layouts: none -> 1.3 us
    reshape x1 -> x0, local copies, waits for them, and re-layouts: 1.29 us -> none  [on_device(): route.reshape(1, row_count)]
where the time goes in v2:
time: 95.1 us; the launch traced here: 94.9 us
  Pallas kernels  93.6 us (98%)
  local copies, waits for them, and re-layouts  1.3 us (1%)
    pallas_call x1, Pallas kernels, on_device(): pl.pallas_call(kernel, out_shape=jax.ShapeDtypeStruct((row_count // 128,...  93.6 us

profile of v2, /device:TPU:13, one launch (start us, length us, event | category | flops | bytes accessed | tf_op | source)
XLA Modules:
  0.0 94.9 jit_solution(8020183121068601873)
XLA Ops:
  0.0 93.6 %shard_map.37 = f32[12,128]{1,0:T(8,128)} custom-call(bf16[1536,768]{1,0:T(8,128)(2,1)} %emb_ref.1, s32[12,128]{1,0:T(8,128)} %bitcast.3, s32[1,1536]{1,0:T(1,128)} %cluster_ref.1), custom_call_target="tpu_custom_call" | custom-call | tf_op jit(solution)/shard_map/pallas_call | solution.py:381
  93.6 1.3 %copy.5 = f32[1536]{0:T(1024)} copy(f32[1536]{0:T(1024)} %bitcast.2) | data formatting | bytes 12288

commit v3 on v2

--- a/solution.py
+++ b/solution.py
@@ -66,11 +66,22 @@
     barrier = pltpu.get_barrier_semaphore()
 
     def greet(i, carry):
-        other = (me + 1 + i) % 128
-        pl.semaphore_signal(barrier, inc=1, device_id=(other // 4, other % 4), device_id_type=MESH)
-        return carry
-
-    lax.fori_loop(0, 127, greet, 0)
+        other = ((me >> 1) + 1 + i) & 63
+        pl.semaphore_signal(barrier, inc=1, device_id=(other >> 1, (other & 1) * 2 + v0), device_id_type=MESH)
+        return carry
+
+    def greet_more(i, carry):
+        x = i & 3
+        to = device_of(x, (i >> 2) & 3, (i >> 4) * 2 + ((core + x) & 1), 1 - v0)
+        pl.semaphore_signal(barrier, inc=1, device_id=to, device_id_type=MESH)
+        return carry
+
+    lax.fori_loop(0, jnp.where(v0 == core, 63, 64), greet, 0)
+    lax.fori_loop(0, 32, greet_more, 0)
+
+    @pl.when(v0 != core)
+    def _():
+        pl.semaphore_signal(barrier, inc=1, device_id=(grp, (blk + 2) % 4), device_id_type=MESH)
 
     values = emb_ref[...].astype(F32)
     unit[...] = (values * lax.rsqrt(jnp.sum(values * values, axis=1, keepdims=True) + 1e-06)).astype(BF16)
@@ -125,7 +136,13 @@
         tally = jnp.where(which == k, below, tally)
     count[...] = tally
 
-    pl.semaphore_wait(barrier, 127)
+    @pl.when(v0 == core)
+    def _():
+        pl.semaphore_wait(barrier, 95)
+
+    @pl.when(v0 != core)
+    def _():
+        pl.semaphore_wait(barrier, 97)
 
     def count_copy(step):
         return pltpu.make_async_remote_copy(
@@ -177,7 +194,7 @@
 
             return inner
 
-        lax.fori_loop(0, 8, send_one, 0)
+        lax.fori_loop(0, 8, send_one, 0, unroll=2)
         return carry
 
     lax.fori_loop(0, WINDOWS, make_window, 0)
@@ -328,7 +345,7 @@
 
             return inner
 
-        lax.fori_loop(0, 16, one, 0)
+        lax.fori_loop(0, 16, one, 0, unroll=4)
         return carry
 
     lax.fori_loop(0, 4, give_back, 0)

time: 95.1 us -> 91.5 us (0.962)
  Pallas kernels: 93.6 us -> 89.2 us
    pallas_call x1, Pallas kernels: 93.6 us -> 89.2 us  [on_device(): pl.pallas_call(kernel, out_shape=jax.ShapeDtypeStruct((row_count // 128,...]
where the time goes in v3:
time: 91.5 us; the launch traced here: 90.5 us
  Pallas kernels  89.2 us (97%)
  local copies, waits for them, and re-layouts  1.3 us (1%)
    pallas_call x1, Pallas kernels, on_device(): pl.pallas_call(kernel, out_shape=jax.ShapeDtypeStruct((row_count // 128,...  89.2 us

profile of v3, /device:TPU:13, one launch (start us, length us, event | category | flops | bytes accessed | tf_op | source)
XLA Modules:
  0.0 90.5 jit_solution(4286729607625608173)
XLA Ops:
  0.0 89.2 %shard_map.37 = f32[12,128]{1,0:T(8,128)} custom-call(bf16[1536,768]{1,0:T(8,128)(2,1)} %emb_ref.1, s32[12,128]{1,0:T(8,128)} %bitcast.3, s32[1,1536]{1,0:T(1,128)} %cluster_ref.1), custom_call_target="tpu_custom_call" | custom-call | tf_op jit(solution)/shard_map/pallas_call | solution.py:398
  89.2 1.3 %copy.5 = f32[1536]{0:T(1024)} copy(f32[1536]{0:T(1024)} %bitcast.2) | data formatting | bytes 12288

commit v4 on v3

--- a/solution.py
+++ b/solution.py
@@ -76,11 +76,12 @@
         pl.semaphore_signal(barrier, inc=1, device_id=to, device_id_type=MESH)
         return carry
 
-    lax.fori_loop(0, jnp.where(v0 == core, 63, 64), greet, 0)
-    lax.fori_loop(0, 32, greet_more, 0)
+    lax.fori_loop(0, 63, greet, 0, unroll=9)
+    lax.fori_loop(0, 32, greet_more, 0, unroll=8)
 
     @pl.when(v0 != core)
     def _():
+        greet(63, 0)
         pl.semaphore_signal(barrier, inc=1, device_id=(grp, (blk + 2) % 4), device_id_type=MESH)
 
     values = emb_ref[...].astype(F32)
@@ -194,7 +195,7 @@
 
             return inner
 
-        lax.fori_loop(0, 8, send_one, 0, unroll=2)
+        lax.fori_loop(0, 8, send_one, 0, unroll=4)
         return carry
 
     lax.fori_loop(0, WINDOWS, make_window, 0)

time: 91.5 us -> 91.8 us (level)
  Pallas kernels: 89.2 us -> 90.3 us
    pallas_call x1, Pallas kernels: 89.2 us -> 90.3 us  [on_device(): pl.pallas_call(kernel, out_shape=jax.ShapeDtypeStruct((row_count // 128,...]
where the time goes in v4:
time: 91.8 us; the launch traced here: 91.6 us
  Pallas kernels  90.3 us (98%)
  local copies, waits for them, and re-layouts  1.3 us (1%)
    pallas_call x1, Pallas kernels, on_device(): pl.pallas_call(kernel, out_shape=jax.ShapeDtypeStruct((row_count // 128,...  90.3 us

profile of v4, /device:TPU:13, one launch (start us, length us, event | category | flops | bytes accessed | tf_op | source)
XLA Modules:
  0.0 91.6 jit_solution(15001194019499598341)
XLA Ops:
  0.0 90.3 %shard_map.37 = f32[12,128]{1,0:T(8,128)} custom-call(bf16[1536,768]{1,0:T(8,128)(2,1)} %emb_ref.1, s32[12,128]{1,0:T(8,128)} %bitcast.3, s32[1,1536]{1,0:T(1,128)} %cluster_ref.1), custom_call_target="tpu_custom_call" | custom-call | tf_op jit(solution)/shard_map/pallas_call | solution.py:399
  90.3 1.3 %copy.5 = f32[1536]{0:T(1024)} copy(f32[1536]{0:T(1024)} %bitcast.2) | data formatting | bytes 12288
